TPU v7x, 32 devices: a whole 2x2x4 slice. The times are simulated.
32 devices in a mesh: depth: 2 (over y), row: 4 (over z), col: 4 (over x, core).
Axes of the slice: x: 2, y: 2, z: 4, core: 2. Of those that a mesh axis runs over, the one named last changes fastest.
Arguments:
- prop: bfloat16 [2, 2, 8192, 8192], P('depth', None, 'row', 'col'), may hold values from -0.046875 to 0.046875
- source: float32 [8192, 256], P(('row', 'col')), may hold values from -6 to 6
- down_init: float32 [2, 8192, 256], P('depth', ('row', 'col')), may hold values from -6 to 6
- up_init: float32 [2, 8192, 256], P('depth', ('row', 'col')), may hold values from -6 to 6
- refl_down: float32 [2, 8192], P('depth', ('row', 'col')), may hold values from -0.6 to 0.6
- refl_up: float32 [2, 8192], P('depth', ('row', 'col')), may hold values from -0.6 to 0.6
Outputs:
- down_field: float32 [2, 8192, 256], P('depth', ('row', 'col'))
- up_field: float32 [2, 8192, 256], P('depth', ('row', 'col'))
All inputs are finite; a program needn't handle non-finite values.
Results may differ from a plain program's by a relative error of at most 0.0041.
Values may be sent and summed in bfloat16 or wider, within the bound.
No kernel may reach another device: no remote copies, remote signals or barrier semaphores. Data moves between devices by JAX's collectives and lax.ppermute only.
A program may use at most 64 MiB of HBM per device.

v0:
```python
import jax
import jax.numpy as jnp
from jax import lax
from jax.sharding import PartitionSpec as P

PASSES = 2


def passed_along(x, axis, by):
    peers = lax.axis_size(axis)
    pairs = [(i, i + by) for i in range(peers) if 0 <= i + by < peers]
    return lax.ppermute(x, axis, pairs)


def complex_join(first, second, sources):
    real_part = first[:, :sources] - second[:, sources:]
    imag_part = first[:, sources:] + second[:, :sources]
    return jnp.concatenate([real_part, imag_part], axis=1)


def downward(weight_real, weight_imag, down_low, sources):
    gathered = lax.all_gather(down_low, "row", axis=0, tiled=True)
    return lax.psum_scatter(
        complex_join(
            jnp.dot(weight_real, gathered, preferred_element_type=jnp.float32),
            jnp.dot(weight_imag, gathered, preferred_element_type=jnp.float32),
            sources,
        ),
        "col",
        scatter_dimension=0,
        tiled=True,
    )


def upward(weight_real, weight_imag, up_low, sources):
    gathered = lax.all_gather(up_low, "col", axis=0, tiled=True)
    numbers = (((0,), (0,)), ((), ()))
    first = lax.dot_general(weight_real, gathered, numbers, preferred_element_type=jnp.float32)
    second = lax.dot_general(weight_imag, gathered, numbers, preferred_element_type=jnp.float32)
    return lax.psum_scatter(
        complex_join(first, second, sources), "row", scatter_dimension=0, tiled=True
    )


def send_trans(trans):
    return passed_along(trans, "depth", 1)


def send_back(back):
    return passed_along(back, "depth", -1)


def body(prop, source, down_init, up_init, refl_down, refl_up):
    weight_real = prop[0, 0]
    weight_imag = prop[0, 1]
    sources = down_init.shape[2] // 2
    at_surface = lax.axis_index("depth") == 0
    refl_above = refl_down[0][:, None]
    refl_below = refl_up[0][:, None]
    down = down_init[0]
    up = up_init[0]
    for sweep in range(PASSES):
        down_low = down.astype(jnp.bfloat16)
        up_low = up.astype(jnp.bfloat16)
        trans = downward(weight_real, weight_imag, down_low, sources)
        from_above = send_trans(trans)
        back = upward(weight_real, weight_imag, up_low, sources)
        from_below = send_back(back)
        above = jnp.where(at_surface, source, from_above)
        down = above + refl_above * back
        up = from_below + refl_below * trans
    return (down[None], up[None])


def solution(mesh):
    placed = (
        P("depth", None, "row", "col"),
        P(("row", "col"), None),
        P("depth", ("row", "col"), None),
        P("depth", ("row", "col"), None),
        P("depth", ("row", "col")),
        P("depth", ("row", "col")),
    )
    return jax.shard_map(
        body,
        mesh=mesh,
        in_specs=placed,
        out_specs=(P("depth", ("row", "col"), None), P("depth", ("row", "col"), None)),
        check_vma=False,
    )
```

profile of v0, /device:TPU:0, one launch (start us, length us, event | category | flops | bytes accessed | tf_op | source)
XLA Modules:
  0.0 290.8 jit_solution(9658612321237586070)
XLA Ops:
  7.2 1.8 convert_element_type.18
  9.1 1.8 convert_element_type.20
  10.9 29.9 %all-gather.11.cloned.1.call-done = bf16[1,2048,256]{2,1,0:T(8,128)(2,1)} async-done(((bf16[1,512,256]{2,1,0:T(8,128)(2,1)}), bf16[1,2048,256]{2,1,0:T(8,128)(2,1)}) %all-gather.11.cloned.1.call-update) | async-done | bytes 1048592 | tf_op jit(solution)/shard_map/all_gather | solution.py:22
  40.8 6.1 %fusion.6 = f32[2048,256]{0,1:T(8,128)S(1)} fusion(bf16[1,2,2048,2048]{3,2,1,0:T(8,128)(2,1)} %param.6, bf16[1,2048,256]{2,1,0:T(8,128)(2,1)} %all-gather.11.cloned.1.call-done), kind=kOutput, calls=%fused_computation.6 | convolution fusion | flops 2147483648 | bytes 11534336 | tf_op jit(solution)/shard_map/dot_general | solution.py:26
  47.0 2.4 copy-done.6
  49.6 2.4 fusion.14
  53.9 5.3 %all-gather.13.cloned.1.call-done = bf16[1,2048,256]{2,1,0:T(8,128)(2,1)} async-done(((bf16[1,512,256]{2,1,0:T(8,128)(2,1)}), bf16[1,2048,256]{2,1,0:T(8,128)(2,1)}) %all-gather.13.cloned.1.call-update) | async-done | bytes 1048592 | tf_op jit(solution)/shard_map/all_gather | solution.py:36
  59.2 6.1 %fusion.4 = f32[2048,256]{0,1:T(8,128)S(1)} fusion(bf16[1,2,2048,2048]{3,2,1,0:T(8,128)(2,1)} %param.6, bf16[1,2048,256]{2,1,0:T(8,128)(2,1)} %all-gather.13.cloned.1.call-done), kind=kOutput, calls=%fused_computation.4 | convolution fusion | flops 2147483648 | bytes 11534336 | tf_op jit(solution)/shard_map/dot_general | solution.py:39
  65.3 6.1 %fusion.12 = f32[2048,256]{0,1:T(8,128)S(1)} fusion(bf16[1,2,2048,2048]{3,2,1,0:T(8,128)(2,1)} %param.6, bf16[1,2048,256]{2,1,0:T(8,128)(2,1)S(1)} %copy-done.7), kind=kOutput, calls=%fused_computation.12 | convolution fusion | flops 2147483648 | bytes 11534336 | tf_op jit(solution)/shard_map/dot_general | solution.py:38
  73.2 20.0 %reduce-scatter.5.cloned.1.call-done = f32[512,256]{0,1:T(8,128)} async-done(((f32[2048,256]{0,1:T(8,128)}), f32[512,256]{0,1:T(8,128)}) %reduce-scatter.5.cloned.1.call-update) | async-done | bytes 524304 | tf_op jit(solution)/shard_map/reduce_scatter | solution.py:23
  93.2 3.5 %collective-permute-start = (f32[512,256]{0,1:T(8,128)}, f32[512,256]{0,1:T(8,128)S(1)}, u32[]{:S(2)}, u32[]{:S(2)}) collective-permute-start(f32[512,256]{0,1:T(8,128)} %reduce-scatter.5.cloned.1.call-done), channel_id=1, source_target_pairs={{0,16},{1,17},{2,18},{3,19},{4,20},{5,21},{6,22},{7,23},{8,24},{9,... | collective-permute-start | bytes 1572872 | tf_op jit(solution)/shard_map/ppermute | solution.py:12
  96.9 42.4 %reduce-scatter.7.cloned.1.call-done = f32[512,256]{0,1:T(8,128)} async-done(((f32[2048,256]{0,1:T(8,128)}), f32[512,256]{0,1:T(8,128)}) %reduce-scatter.7.cloned.1.call-update) | async-done | bytes 524304 | tf_op jit(solution)/shard_map/reduce_scatter | solution.py:40
  139.3 2.0 add_convert_fusion.1
  142.7 14.1 %collective-permute-done.2 = f32[512,256]{0,1:T(8,128)S(1)} collective-permute-done((f32[512,256]{0,1:T(8,128)S(1)}, f32[512,256]{0,1:T(8,128)S(1)}, u32[]{:S(2)}, u32[]{:S(2)}) %collective-permute-start.2) | collective-permute-done | bytes 524320 | tf_op jit(solution)/shard_map/ppermute | solution.py:12
  157.9 10.9 %all-gather.7.cloned.1.call-done = bf16[2048,256]{0,1:T(8,128)(2,1)} async-done(((bf16[512,256]{0,1:T(8,128)(2,1)}), bf16[2048,256]{0,1:T(8,128)(2,1)}) %all-gather.7.cloned.1.call-update) | async-done | bytes 1048592 | tf_op jit(solution)/shard_map/all_gather | solution.py:22
  168.8 6.1 %fusion.30 = f32[2048,256]{0,1:T(8,128)S(1)} fusion(bf16[2048,256]{0,1:T(8,128)(2,1)} %all-gather.7.cloned.1.call-done, bf16[1,2,2048,2048]{3,2,1,0:T(8,128)(2,1)} %param.6), kind=kOutput, calls=%fused_computation.26 | convolution fusion | flops 2147483648 | bytes 11534336 | tf_op jit(solution)/shard_map/dot_general | solution.py:26
  174.9 6.1 %fusion.24 = f32[2048,256]{0,1:T(8,128)S(1)} fusion(bf16[2048,256]{0,1:T(8,128)(2,1)S(1)} %copy-done.9, bf16[1,2,2048,2048]{3,2,1,0:T(8,128)(2,1)} %param.6), kind=kOutput, calls=%fused_computation.24 | convolution fusion | flops 2147483648 | bytes 11534336 | tf_op jit(solution)/shard_map/dot_general | solution.py:25
  182.9 4.1 %all-gather.9.cloned.1.call-done = bf16[2048,256]{0,1:T(8,128)(2,1)} async-done(((bf16[512,256]{0,1:T(8,128)(2,1)}), bf16[2048,256]{0,1:T(8,128)(2,1)}) %all-gather.9.cloned.1.call-update) | async-done | bytes 1048592 | tf_op jit(solution)/shard_map/all_gather | solution.py:36
  187.0 6.1 %fusion.33 = f32[2048,256]{0,1:T(8,128)S(1)} fusion(bf16[2048,256]{0,1:T(8,128)(2,1)} %all-gather.9.cloned.1.call-done, bf16[1,2,2048,2048]{3,2,1,0:T(8,128)(2,1)} %param.6), kind=kOutput, calls=%fused_computation.27 | convolution fusion | flops 2147483648 | bytes 11534336 | tf_op jit(solution)/shard_map/dot_general | solution.py:39
  193.1 6.1 %fusion.27 = f32[2048,256]{0,1:T(8,128)S(1)} fusion(bf16[2048,256]{0,1:T(8,128)(2,1)S(1)} %copy-done.8, bf16[1,2,2048,2048]{3,2,1,0:T(8,128)(2,1)} %param.6), kind=kOutput, calls=%fused_computation.25 | convolution fusion | flops 2147483648 | bytes 11534336 | tf_op jit(solution)/shard_map/dot_general | solution.py:38
  201.1 19.9 %reduce-scatter.9.cloned.1.call-done = f32[512,256]{0,1:T(8,128)} async-done(((f32[2048,256]{0,1:T(8,128)}), f32[512,256]{0,1:T(8,128)}) %reduce-scatter.9.cloned.1.call-update) | async-done | bytes 524304 | tf_op jit(solution)/shard_map/reduce_scatter | solution.py:23
  221.0 3.6 %collective-permute-start.1 = (f32[512,256]{0,1:T(8,128)}, f32[512,256]{0,1:T(8,128)S(1)}, u32[]{:S(2)}, u32[]{:S(2)}) collective-permute-start(f32[512,256]{0,1:T(8,128)} %reduce-scatter.9.cloned.1.call-done), channel_id=1, source_target_pairs={{0,16},{1,17},{2,18},{3,19},{4,20},{5,21},{6,22},{7,23},{8,24},{9,... | collective-permute-start | bytes 1572872 | tf_op jit(solution)/shard_map/ppermute | solution.py:12
  224.6 42.8 %reduce-scatter.11.cloned.1.call-done = f32[512,256]{0,1:T(8,128)} async-done(((f32[2048,256]{0,1:T(8,128)}), f32[512,256]{0,1:T(8,128)}) %reduce-scatter.11.cloned.1.call-update) | async-done | bytes 524304 | tf_op jit(solution)/shard_map/reduce_scatter | solution.py:40
  270.8 12.1 %collective-permute-done.3 = f32[512,256]{0,1:T(8,128)S(1)} collective-permute-done((f32[512,256]{0,1:T(8,128)}, f32[512,256]{0,1:T(8,128)S(1)}, u32[]{:S(2)}, u32[]{:S(2)}) %collective-permute-start.3) | collective-permute-done | bytes 524320 | tf_op jit(solution)/shard_map/ppermute | solution.py:12
  (55 shorter events, 14.8 us)
Async XLA Ops:
  7.2 33.6 %all-gather.11.cloned.1.call-start = ((), (), s32[]{:S(2)}) async-start(), calls=%async_computation.10 | async-start | bytes 1310720 | tf_op jit(solution)/shard_map/all_gather | solution.py:22
  9.0 50.2 %all-gather.13.cloned.1.call-start = ((), (), s32[]{:S(2)}) async-start(), calls=%async_computation.11 | async-start | bytes 1310720 | tf_op jit(solution)/shard_map/all_gather | solution.py:36
  10.9 82.3 %reduce-scatter.5.cloned.1.call-start = ((), (), s32[]{:S(2)}) async-start(), calls=%async_computation.4 | async-start | bytes 2621440 | tf_op jit(solution)/shard_map/reduce_scatter | solution.py:23
  40.8 8.6 %copy-start.6 = (bf16[1,2,2048,2048]{3,2,1,0:T(8,128)(2,1)S(1)}, bf16[1,2,2048,2048]{3,2,1,0:T(8,128)(2,1)}, u32[]{:S(2)}) copy-start(bf16[1,2,2048,2048]{3,2,1,0:T(8,128)(2,1)} %param.6) | copy-start | bytes 50331652
  40.8 8.8 %copy-start.10 = (bf16[1,2048,256]{2,1,0:T(8,128)(2,1)S(1)}, bf16[1,2048,256]{2,1,0:T(8,128)(2,1)}, u32[]{:S(2)}) copy-start(bf16[1,2048,256]{2,1,0:T(8,128)(2,1)} %all-gather.11.cloned.1.call-done) | copy-start | bytes 3145732
  53.8 85.5 %reduce-scatter.7.cloned.1.call-start = ((), (), s32[]{:S(2)}) async-start(), calls=%async_computation.5 | async-start | bytes 2621440 | tf_op jit(solution)/shard_map/reduce_scatter | solution.py:40
  59.2 6.1 %copy-start.7 = (bf16[1,2048,256]{2,1,0:T(8,128)(2,1)S(1)}, bf16[1,2048,256]{2,1,0:T(8,128)(2,1)}, u32[]{:S(2)}) copy-start(bf16[1,2048,256]{2,1,0:T(8,128)(2,1)} %all-gather.13.cloned.1.call-done) | copy-start | bytes 3145732
  73.1 23.6 %copy-start.2 = (f32[512,256]{1,0:T(8,128)S(1)}, f32[512,256]{1,0:T(8,128)}, u32[]{:S(2)}) copy-start(f32[512,256]{1,0:T(8,128)} %param.7) | copy-start | bytes 1572868
  73.1 66.2 %copy-start.5 = (f32[1,512]{1,0:T(1,128)S(1)}, f32[1,512]{1,0:T(1,128)}, u32[]{:S(2)}) copy-start(f32[1,512]{1,0:T(1,128)} %param.10) | copy-start | bytes 6148
  73.2 83.7 %copy-start.4 = (f32[1,512]{1,0:T(1,128)S(1)}, f32[1,512]{1,0:T(1,128)}, u32[]{:S(2)}) copy-start(f32[1,512]{1,0:T(1,128)} %param.11) | copy-start | bytes 6148
  73.2 95.6 %all-gather.7.cloned.1.call-start = ((), (), s32[]{:S(2)}) async-start(), calls=%async_computation.6 | async-start | bytes 1310720 | tf_op jit(solution)/shard_map/all_gather | solution.py:22
  93.2 63.6 %copy-start = (f32[512,256]{0,1:T(8,128)S(1)}, f32[512,256]{0,1:T(8,128)}, u32[]{:S(2)}) copy-start(f32[512,256]{0,1:T(8,128)} %reduce-scatter.5.cloned.1.call-done) | copy-start | bytes 1572868
  93.2 46.2 %collective-permute-start = (f32[512,256]{0,1:T(8,128)}, f32[512,256]{0,1:T(8,128)S(1)}, u32[]{:S(2)}, u32[]{:S(2)}) collective-permute-start(f32[512,256]{0,1:T(8,128)} %reduce-scatter.5.cloned.1.call-done), channel_id=1, source_target_pairs={{0,16},{1,17},{2,18},{3,19},{4,20},{5,21},{6,22},{7,23},{8,24},{9,... | collective-permute-start | bytes 1572872 | tf_op jit(solution)/shard_map/ppermute | solution.py:12
  139.3 2.1 copy-start.1
  141.3 45.7 %all-gather.9.cloned.1.call-start = ((), (), s32[]{:S(2)}) async-start(), calls=%async_computation.8 | async-start | bytes 1310720 | tf_op jit(solution)/shard_map/all_gather | solution.py:36
  141.4 15.4 %collective-permute-start.2 = (f32[512,256]{0,1:T(8,128)S(1)}, f32[512,256]{0,1:T(8,128)S(1)}, u32[]{:S(2)}, u32[]{:S(2)}) collective-permute-start(f32[512,256]{0,1:T(8,128)S(1)} %copy-done.1), channel_id=1, source_target_pairs={{16,0},{17,1},{18,2},{19,3},{20,4},{21,5},{22,6},{23,7},{24,8},{25... | collective-permute-start | bytes 1572872 | tf_op jit(solution)/shard_map/ppermute | solution.py:12
  157.7 63.3 %reduce-scatter.9.cloned.1.call-start = ((), (), s32[]{:S(2)}) async-start(), calls=%async_computation.7 | async-start | bytes 2621440 | tf_op jit(solution)/shard_map/reduce_scatter | solution.py:23
  168.8 6.2 %copy-start.9 = (bf16[2048,256]{0,1:T(8,128)(2,1)S(1)}, bf16[2048,256]{0,1:T(8,128)(2,1)}, u32[]{:S(2)}) copy-start(bf16[2048,256]{0,1:T(8,128)(2,1)} %all-gather.7.cloned.1.call-done) | copy-start | bytes 3145732
  182.8 84.5 %reduce-scatter.11.cloned.1.call-start = ((), (), s32[]{:S(2)}) async-start(), calls=%async_computation.9 | async-start | bytes 2621440 | tf_op jit(solution)/shard_map/reduce_scatter | solution.py:40
  187.0 6.1 %copy-start.8 = (bf16[2048,256]{0,1:T(8,128)(2,1)S(1)}, bf16[2048,256]{0,1:T(8,128)(2,1)}, u32[]{:S(2)}) copy-start(bf16[2048,256]{0,1:T(8,128)(2,1)} %all-gather.9.cloned.1.call-done) | copy-start | bytes 3145732
  221.0 61.9 %copy-start.3 = (f32[512,256]{0,1:T(8,128)S(1)}, f32[512,256]{0,1:T(8,128)}, u32[]{:S(2)}) copy-start(f32[512,256]{0,1:T(8,128)} %reduce-scatter.9.cloned.1.call-done) | copy-start | bytes 1572868
  221.0 47.6 %collective-permute-start.1 = (f32[512,256]{0,1:T(8,128)}, f32[512,256]{0,1:T(8,128)S(1)}, u32[]{:S(2)}, u32[]{:S(2)}) collective-permute-start(f32[512,256]{0,1:T(8,128)} %reduce-scatter.9.cloned.1.call-done), channel_id=1, source_target_pairs={{0,16},{1,17},{2,18},{3,19},{4,20},{5,21},{6,22},{7,23},{8,24},{9,... | collective-permute-start | bytes 1572872 | tf_op jit(solution)/shard_map/ppermute | solution.py:12
  267.3 15.6 %collective-permute-start.3 = (f32[512,256]{0,1:T(8,128)}, f32[512,256]{0,1:T(8,128)S(1)}, u32[]{:S(2)}, u32[]{:S(2)}) collective-permute-start(f32[512,256]{0,1:T(8,128)} %reduce-scatter.11.cloned.1.call-done), channel_id=1, source_target_pairs={{16,0},{17,1},{18,2},{19,3},{20,4},{21,5},{22,6},{23,7},{24,8},{25... | collective-permute-start | bytes 1572872 | tf_op jit(solution)/shard_map/ppermute | solution.py:12
Sparse Core Ops, SparseCore 0:
  10.1 30.6 all-gather.10
  42.9 16.2 all-gather.12
  61.7 31.4 reduce-scatter.4
  95.4 43.8 reduce-scatter.6
  141.5 27.2 all-gather.6
  170.8 16.2 all-gather.8
  189.5 31.4 reduce-scatter.8
  223.4 43.8 reduce-scatter.10
where the time goes:
time: 291 us
  waiting for transfers between devices  202 us (69%)
  matrix products  45.2 us (16%)
  other arithmetic  14.6 us (5%)
  between operations  14.3 us (5%)
  starting transfers between devices  10.2 us (4%)
  local copies, waits for them, and re-layouts  4.91 us (2%)
    reduce_scatter x2, waiting for transfers between devices, upward(): lax.psum_scatter(complex_join(first, second, sources), 'row', scatter_dim...  85.2 us
    all_gather x2, waiting for transfers between devices, downward(): gathered = lax.all_gather(down_low, 'row', axis=0, tiled=True)  40.8 us
    reduce_scatter x2, waiting for transfers between devices, downward(): lax.psum_scatter(complex_join(jnp.dot(weight_real, gathered, preferred_el...  39.9 us
    ppermute x4, waiting for transfers between devices, passed_along(): return lax.ppermute(x, axis, pairs)  26.2 us
    dot_general x2, matrix products, downward(): jnp.dot(weight_imag, gathered, preferred_element_type=jnp.float32)  12.3 us
    dot_general x2, matrix products, upward(): lax.dot_general(weight_real, gathered, numbers, preferred_element_type=jn...  12.3 us
    dot_general x2, matrix products, upward(): lax.dot_general(weight_imag, gathered, numbers, preferred_element_type=jn...  12.2 us
    ppermute x4, starting transfers between devices, passed_along(): return lax.ppermute(x, axis, pairs)  9.66 us
  transfers between devices with their start and end apart: 12, of which 10 were waited for; matrix products, arithmetic and copies ran while one was open for 20% of the time, Pallas kernels for 0%

commit v1 on v0

--- a/solution.py
+++ b/solution.py
@@ -33,7 +33,12 @@
 
 
 def upward(weight_real, weight_imag, up_low, sources):
-    gathered = lax.all_gather(up_low, "col", axis=0, tiled=True)
+    ring = [up_low]
+    for hop in range(3):
+        ring.append(lax.ppermute(ring[-1], "col", [(dev, (dev + 1) % 4) for dev in range(4)]))
+    gathered = jnp.roll(
+        jnp.concatenate(ring[::-1], axis=0), (lax.axis_index("col") + 1) * ring[0].shape[0], axis=0
+    )
     numbers = (((0,), (0,)), ((), ()))
     first = lax.dot_general(weight_real, gathered, numbers, preferred_element_type=jnp.float32)
     second = lax.dot_general(weight_imag, gathered, numbers, preferred_element_type=jnp.float32)

time: 291 us -> 281 us (0.966)
  waiting for transfers between devices: 202 us -> 185 us
  other arithmetic: 14.6 us -> 24.1 us
    ppermute x0 -> x6, waiting for transfers between devices: none -> 24.2 us  [upward(): lax.ppermute(ring[-1], 'col', [(dev, (dev + 1) % 4) for dev in range(4)])]
    reduce_scatter x2, waiting for transfers between devices: 85.2 us -> 63.1 us  [upward(): lax.psum_scatter(complex_join(first, second, sources), 'row', scatter_dim...]
    all_gather x2, waiting for transfers between devices: 40.8 us -> 20.1 us  [downward(): gathered = lax.all_gather(down_low, 'row', axis=0, tiled=True)]
    concatenate x0 -> x2, other arithmetic: none -> 10.9 us  [upward(): jnp.roll(jnp.concatenate(ring[::-1], axis=0), (lax.axis_index('col') + 1)...]
    reduce_scatter x2, waiting for transfers between devices: 39.9 us -> 49.7 us  [downward(): lax.psum_scatter(complex_join(jnp.dot(weight_real, gathered, preferred_el...]
    all_gather x2 -> x0, waiting for transfers between devices: 9.43 us -> none  [upward(): gathered = lax.all_gather(up_low, 'col', axis=0, tiled=True)]
    dot_general x2, matrix products: 12.3 us -> 8.42 us  [upward(): lax.dot_general(weight_real, gathered, numbers, preferred_element_type=jn...]
    dot_general x2, matrix products: 8.52 us -> 12.3 us  [downward(): jnp.dot(weight_real, gathered, preferred_element_type=jnp.float32)]
  transfers between devices with their start and end apart: 12 -> 16, of which waited for: 10 -> 15; matrix products, arithmetic and copies ran while one was open for 20% -> 24% of each run, Pallas kernels for 0% -> 0%
where the time goes in v1:
time: 281 us
  waiting for transfers between devices  185 us (66%)
  matrix products  44.5 us (16%)
  other arithmetic  24.1 us (9%)
  between operations  14.3 us (5%)
  starting transfers between devices  10.7 us (4%)
    reduce_scatter x2, waiting for transfers between devices, upward(): lax.psum_scatter(complex_join(first, second, sources), 'row', scatter_dim...  63.1 us
    reduce_scatter x2, waiting for transfers between devices, downward(): lax.psum_scatter(complex_join(jnp.dot(weight_real, gathered, preferred_el...  49.7 us
    ppermute x4, waiting for transfers between devices, passed_along(): return lax.ppermute(x, axis, pairs)  27.7 us
    ppermute x6, waiting for transfers between devices, upward(): lax.ppermute(ring[-1], 'col', [(dev, (dev + 1) % 4) for dev in range(4)])  24.2 us
    all_gather x2, waiting for transfers between devices, downward(): gathered = lax.all_gather(down_low, 'row', axis=0, tiled=True)  20.1 us
    dot_general x2, matrix products, downward(): jnp.dot(weight_real, gathered, preferred_element_type=jnp.float32)  12.3 us
    dot_general x2, matrix products, downward(): jnp.dot(weight_imag, gathered, preferred_element_type=jnp.float32)  12.2 us
    dot_general x2, matrix products, upward(): lax.dot_general(weight_imag, gathered, numbers, preferred_element_type=jn...  11.5 us
  transfers between devices with their start and end apart: 16, of which 15 were waited for; matrix products, arithmetic and copies ran while one was open for 24% of the time, Pallas kernels for 0%

profile of v1, /device:TPU:0, one launch (start us, length us, event | category | flops | bytes accessed | tf_op | source)
XLA Modules:
  0.0 280.6 jit_solution(16845856645769185137)
XLA Ops:
  8.8 6.0 %collective-permute-done.1 = bf16[512,256]{1,0:T(8,128)(2,1)S(1)} collective-permute-done((bf16[512,256]{1,0:T(8,128)(2,1)S(1)}, bf16[512,256]{1,0:T(8,128)(2,1)S(1)}, u32[]{:S(2)}, u32[]{:S(2)}) %collective-permute-start.1) | collective-permute-done | bytes 262176 | tf_op jit(solution)/shard_map/ppermute | solution.py:38
  14.8 5.8 %collective-permute-done.2 = bf16[512,256]{1,0:T(8,128)(2,1)S(1)} collective-permute-done((bf16[512,256]{1,0:T(8,128)(2,1)S(1)}, bf16[512,256]{1,0:T(8,128)(2,1)S(1)}, u32[]{:S(2)}, u32[]{:S(2)}) %collective-permute-start.2) | collective-permute-done | bytes 262176 | tf_op jit(solution)/shard_map/ppermute | solution.py:38
  22.4 3.9 %collective-permute-done.3 = bf16[512,256]{1,0:T(8,128)(2,1)S(1)} collective-permute-done((bf16[512,256]{1,0:T(8,128)(2,1)S(1)}, bf16[512,256]{1,0:T(8,128)(2,1)S(1)}, u32[]{:S(2)}, u32[]{:S(2)}) %collective-permute-start.3) | collective-permute-done | bytes 262176 | tf_op jit(solution)/shard_map/ppermute | solution.py:38
  26.4 9.6 %fusion.52 = bf16[2048,256]{1,0:T(8,128)(2,1)S(1)} fusion(s32[]{:T(128)S(6)} %select_n.28, bf16[512,256]{1,0:T(8,128)(2,1)S(1)} %collective-permute-done.3, bf16[512,256]{1,0:T(8,128)(2,1)S(1)} %collective-permute-done.2, bf16[512,256]{1,0:T(8,128)(2,1)S(1)} %collective-permute-done.1, bf16[512,256]{1,0:T(8,128)(2,1)S(1)} %convert_bitcast_fusion), kind=kLoop, calls=%fused_computation.60 | loop fusion | flops 8388608 | bytes 2097156 | tf_op jit(solution)/shard_map/jit(_roll_dynamic)/concatenate | solution.py:39
  36.0 5.8 %fusion.33 = f32[2048,256]{0,1:T(8,128)S(1)} fusion(bf16[2048,256]{1,0:T(8,128)(2,1)S(1)} %fusion.52, bf16[1,2,2048,2048]{3,2,1,0:T(8,128)(2,1)} %param.8), kind=kOutput, calls=%fused_computation.27 | convolution fusion | flops 2147483648 | bytes 11534336 | tf_op jit(solution)/shard_map/dot_general | solution.py:44
  41.7 2.5 fusion.24
  46.2 6.7 %all-gather.6.cloned.1.call-done = bf16[1,2048,256]{2,1,0:T(8,128)(2,1)} async-done(((bf16[1,512,256]{2,1,0:T(8,128)(2,1)}), bf16[1,2048,256]{2,1,0:T(8,128)(2,1)}) %all-gather.6.cloned.1.call-update) | async-done | bytes 1048592 | tf_op jit(solution)/shard_map/all_gather | solution.py:22
  52.8 6.1 %fusion.6 = f32[2048,256]{0,1:T(8,128)S(1)} fusion(bf16[1,2,2048,2048]{3,2,1,0:T(8,128)(2,1)} %param.8, bf16[1,2048,256]{2,1,0:T(8,128)(2,1)} %all-gather.6.cloned.1.call-done), kind=kOutput, calls=%fused_computation.6 | convolution fusion | flops 2147483648 | bytes 11534336 | tf_op jit(solution)/shard_map/dot_general | solution.py:26
  58.9 6.2 %fusion.14 = f32[2048,256]{0,1:T(8,128)S(1)} fusion(bf16[1,2,2048,2048]{3,2,1,0:T(8,128)(2,1)} %param.8, bf16[1,2048,256]{2,1,0:T(8,128)(2,1)S(1)} %copy-done.6), kind=kOutput, calls=%fused_computation.14 | convolution fusion | flops 2147483648 | bytes 11534336 | tf_op jit(solution)/shard_map/dot_general | solution.py:25
  66.9 31.6 %reduce-scatter.7.cloned.1.call-done = f32[512,256]{0,1:T(8,128)} async-done(((f32[2048,256]{0,1:T(8,128)}), f32[512,256]{0,1:T(8,128)}) %reduce-scatter.7.cloned.1.call-update) | async-done | bytes 524304 | tf_op jit(solution)/shard_map/reduce_scatter | solution.py:45
  99.9 14.3 %collective-permute-done.5 = f32[512,256]{0,1:T(8,128)S(1)} collective-permute-done((f32[512,256]{0,1:T(8,128)}, f32[512,256]{0,1:T(8,128)S(1)}, u32[]{:S(2)}, u32[]{:S(2)}) %collective-permute-start.5) | collective-permute-done | bytes 524320 | tf_op jit(solution)/shard_map/ppermute | solution.py:12
  114.2 17.8 %reduce-scatter.5.cloned.1.call-done = f32[512,256]{0,1:T(8,128)} async-done(((f32[2048,256]{0,1:T(8,128)}), f32[512,256]{0,1:T(8,128)}) %reduce-scatter.5.cloned.1.call-update) | async-done | bytes 524304 | tf_op jit(solution)/shard_map/reduce_scatter | solution.py:23
  133.2 3.4 %collective-permute-start = (f32[512,256]{0,1:T(8,128)}, f32[512,256]{0,1:T(8,128)S(1)}, u32[]{:S(2)}, u32[]{:S(2)}) collective-permute-start(f32[512,256]{0,1:T(8,128)} %reduce-scatter.5.cloned.1.call-done), channel_id=1, source_target_pairs={{0,16},{1,17},{2,18},{3,19},{4,20},{5,21},{6,22},{7,23},{8,24},{9,... | collective-permute-start | bytes 1572872 | tf_op jit(solution)/shard_map/ppermute | solution.py:12
  139.2 5.6 %collective-permute-done.7 = bf16[512,256]{0,1:T(8,128)(2,1)S(1)} collective-permute-done((bf16[512,256]{0,1:T(8,128)(2,1)S(1)}, bf16[512,256]{0,1:T(8,128)(2,1)S(1)}, u32[]{:S(2)}, u32[]{:S(2)}) %collective-permute-start.7) | collective-permute-done | bytes 262176 | tf_op jit(solution)/shard_map/ppermute | solution.py:38
  144.8 4.1 %collective-permute-done = f32[512,256]{0,1:T(8,128)S(1)} collective-permute-done((f32[512,256]{0,1:T(8,128)}, f32[512,256]{0,1:T(8,128)S(1)}, u32[]{:S(2)}, u32[]{:S(2)}) %collective-permute-start) | collective-permute-done | bytes 524320 | tf_op jit(solution)/shard_map/ppermute | solution.py:12
  151.9 5.7 %fusion.39 = f32[2048,256]{0,1:T(8,128)S(1)} fusion(bf16[2048,256]{0,1:T(8,128)(2,1)S(1)} %fusion.45, bf16[1,2,2048,2048]{3,2,1,0:T(8,128)(2,1)} %param.8), kind=kOutput, calls=%fused_computation.29 | convolution fusion | flops 2147483648 | bytes 11534336 | tf_op jit(solution)/shard_map/dot_general | solution.py:44
  157.7 5.9 %fusion.30 = f32[2048,256]{0,1:T(8,128)S(1)} fusion(bf16[2048,256]{0,1:T(8,128)(2,1)S(1)} %fusion.45, bf16[1,2,2048,2048]{3,2,1,0:T(8,128)(2,1)} %param.8), kind=kOutput, calls=%fused_computation.26 | convolution fusion | flops 2147483648 | bytes 11534336 | tf_op jit(solution)/shard_map/dot_general | solution.py:43
  165.4 13.4 %all-gather.4.cloned.1.call-done = bf16[2048,256]{0,1:T(8,128)(2,1)} async-done(((bf16[512,256]{0,1:T(8,128)(2,1)}), bf16[2048,256]{0,1:T(8,128)(2,1)}) %all-gather.4.cloned.1.call-update) | async-done | bytes 1048592 | tf_op jit(solution)/shard_map/all_gather | solution.py:22
  178.9 6.1 %fusion.36 = f32[2048,256]{0,1:T(8,128)S(1)} fusion(bf16[2048,256]{0,1:T(8,128)(2,1)} %all-gather.4.cloned.1.call-done, bf16[1,2,2048,2048]{3,2,1,0:T(8,128)(2,1)} %param.8), kind=kOutput, calls=%fused_computation.28 | convolution fusion | flops 2147483648 | bytes 11534336 | tf_op jit(solution)/shard_map/dot_general | solution.py:26
  185.0 6.1 %fusion.27 = f32[2048,256]{0,1:T(8,128)S(1)} fusion(bf16[2048,256]{0,1:T(8,128)(2,1)S(1)} %copy-done.7, bf16[1,2,2048,2048]{3,2,1,0:T(8,128)(2,1)} %param.8), kind=kOutput, calls=%fused_computation.25 | convolution fusion | flops 2147483648 | bytes 11534336 | tf_op jit(solution)/shard_map/dot_general | solution.py:25
  192.9 31.5 %reduce-scatter.11.cloned.1.call-done = f32[512,256]{0,1:T(8,128)} async-done(((f32[2048,256]{0,1:T(8,128)}), f32[512,256]{0,1:T(8,128)}) %reduce-scatter.11.cloned.1.call-update) | async-done | bytes 524304 | tf_op jit(solution)/shard_map/reduce_scatter | solution.py:45
  225.8 31.9 %reduce-scatter.9.cloned.1.call-done = f32[512,256]{0,1:T(8,128)} async-done(((f32[2048,256]{0,1:T(8,128)}), f32[512,256]{0,1:T(8,128)}) %reduce-scatter.9.cloned.1.call-update) | async-done | bytes 524304 | tf_op jit(solution)/shard_map/reduce_scatter | solution.py:23
  257.7 3.4 %collective-permute-start.4 = (f32[512,256]{0,1:T(8,128)}, f32[512,256]{0,1:T(8,128)S(1)}, u32[]{:S(2)}, u32[]{:S(2)}) collective-permute-start(f32[512,256]{0,1:T(8,128)} %reduce-scatter.9.cloned.1.call-done), channel_id=1, source_target_pairs={{0,16},{1,17},{2,18},{3,19},{4,20},{5,21},{6,22},{7,23},{8,24},{9,... | collective-permute-start | bytes 1572872 | tf_op jit(solution)/shard_map/ppermute | solution.py:12
  263.3 9.3 %collective-permute-done.4 = f32[512,256]{0,1:T(8,128)S(1)} collective-permute-done((f32[512,256]{0,1:T(8,128)}, f32[512,256]{0,1:T(8,128)S(1)}, u32[]{:S(2)}, u32[]{:S(2)}) %collective-permute-start.4) | collective-permute-done | bytes 524320 | tf_op jit(solution)/shard_map/ppermute | solution.py:12
  (57 shorter events, 23.6 us)
Async XLA Ops:
  7.2 45.7 %all-gather.6.cloned.1.call-start = ((), (), s32[]{:S(2)}) async-start(), calls=%async_computation.9 | async-start | bytes 1310720 | tf_op jit(solution)/shard_map/all_gather | solution.py:22
  8.3 6.5 %collective-permute-start.1 = (bf16[512,256]{1,0:T(8,128)(2,1)S(1)}, bf16[512,256]{1,0:T(8,128)(2,1)S(1)}, u32[]{:S(2)}, u32[]{:S(2)}) collective-permute-start(bf16[512,256]{1,0:T(8,128)(2,1)S(1)} %convert_bitcast_fusion), channel_id=1, source_target_pairs={{0,1},{1,2},{2,3},{3,0},{4,5},{5,6},{6,7},{7,4},{8,9},{9,10},{10,1... | collective-permute-start | bytes 786440 | tf_op jit(solution)/shard_map/ppermute | solution.py:38
  14.8 5.8 %collective-permute-start.2 = (bf16[512,256]{1,0:T(8,128)(2,1)S(1)}, bf16[512,256]{1,0:T(8,128)(2,1)S(1)}, u32[]{:S(2)}, u32[]{:S(2)}) collective-permute-start(bf16[512,256]{1,0:T(8,128)(2,1)S(1)} %collective-permute-done.1), channel_id=1, source_target_pairs={{0,1},{1,2},{2,3},{3,0},{4,5},{5,6},{6,7},{7,4},{8,9},{9,10},{10,1... | collective-permute-start | bytes 786440 | tf_op jit(solution)/shard_map/ppermute | solution.py:38
  20.6 5.8 %collective-permute-start.3 = (bf16[512,256]{1,0:T(8,128)(2,1)S(1)}, bf16[512,256]{1,0:T(8,128)(2,1)S(1)}, u32[]{:S(2)}, u32[]{:S(2)}) collective-permute-start(bf16[512,256]{1,0:T(8,128)(2,1)S(1)} %collective-permute-done.2), channel_id=1, source_target_pairs={{0,1},{1,2},{2,3},{3,0},{4,5},{5,6},{6,7},{7,4},{8,9},{9,10},{10,1... | collective-permute-start | bytes 786440 | tf_op jit(solution)/shard_map/ppermute | solution.py:38
  22.4 76.2 %reduce-scatter.7.cloned.1.call-start = ((), (), s32[]{:S(2)}) async-start(), calls=%async_computation.5 | async-start | bytes 2621440 | tf_op jit(solution)/shard_map/reduce_scatter | solution.py:45
  26.4 15.4 %copy-start.5 = (bf16[1,2,2048,2048]{3,2,1,0:T(8,128)(2,1)S(1)}, bf16[1,2,2048,2048]{3,2,1,0:T(8,128)(2,1)}, u32[]{:S(2)}) copy-start(bf16[1,2,2048,2048]{3,2,1,0:T(8,128)(2,1)} %param.8) | copy-start | bytes 50331652
  46.1 85.9 %reduce-scatter.5.cloned.1.call-start = ((), (), s32[]{:S(2)}) async-start(), calls=%async_computation.4 | async-start | bytes 2621440 | tf_op jit(solution)/shard_map/reduce_scatter | solution.py:23
  52.8 6.1 %copy-start.6 = (bf16[1,2048,256]{2,1,0:T(8,128)(2,1)S(1)}, bf16[1,2048,256]{2,1,0:T(8,128)(2,1)}, u32[]{:S(2)}) copy-start(bf16[1,2048,256]{2,1,0:T(8,128)(2,1)} %all-gather.6.cloned.1.call-done) | copy-start | bytes 3145732
  66.8 65.2 %copy-start.3 = (f32[1,512]{1,0:T(1,128)S(1)}, f32[1,512]{1,0:T(1,128)}, u32[]{:S(2)}) copy-start(f32[1,512]{1,0:T(1,128)} %param.13) | copy-start | bytes 6148
  66.8 72.2 %copy-start.1 = (f32[512,256]{1,0:T(8,128)S(1)}, f32[512,256]{1,0:T(8,128)}, u32[]{:S(2)}) copy-start(f32[512,256]{1,0:T(8,128)} %param.9) | copy-start | bytes 1572868
  66.8 82.1 %copy-start.4 = (f32[1,512]{1,0:T(1,128)S(1)}, f32[1,512]{1,0:T(1,128)}, u32[]{:S(2)}) copy-start(f32[1,512]{1,0:T(1,128)} %param.12) | copy-start | bytes 6148
  66.8 112.0 %all-gather.4.cloned.1.call-start = ((), (), s32[]{:S(2)}) async-start(), calls=%async_computation.6 | async-start | bytes 1310720 | tf_op jit(solution)/shard_map/all_gather | solution.py:22
  98.5 50.4 %copy-start = (f32[512,256]{0,1:T(8,128)S(1)}, f32[512,256]{0,1:T(8,128)}, u32[]{:S(2)}) copy-start(f32[512,256]{0,1:T(8,128)} %reduce-scatter.7.cloned.1.call-done) | copy-start | bytes 1572868
  98.5 15.7 %collective-permute-start.5 = (f32[512,256]{0,1:T(8,128)}, f32[512,256]{0,1:T(8,128)S(1)}, u32[]{:S(2)}, u32[]{:S(2)}) collective-permute-start(f32[512,256]{0,1:T(8,128)} %reduce-scatter.7.cloned.1.call-done), channel_id=1, source_target_pairs={{16,0},{17,1},{18,2},{19,3},{20,4},{21,5},{22,6},{23,7},{24,8},{25... | collective-permute-start | bytes 1572872 | tf_op jit(solution)/shard_map/ppermute | solution.py:12
  133.2 5.8 %collective-permute-start.6 = (bf16[512,256]{0,1:T(8,128)(2,1)S(1)}, bf16[512,256]{0,1:T(8,128)(2,1)S(1)}, u32[]{:S(2)}, u32[]{:S(2)}) collective-permute-start(bf16[512,256]{0,1:T(8,128)(2,1)S(1)} %add_convert_fusion), channel_id=1, source_target_pairs={{0,1},{1,2},{2,3},{3,0},{4,5},{5,6},{6,7},{7,4},{8,9},{9,10},{10,1... | collective-permute-start | bytes 786440 | tf_op jit(solution)/shard_map/ppermute | solution.py:38
  133.2 15.7 %collective-permute-start = (f32[512,256]{0,1:T(8,128)}, f32[512,256]{0,1:T(8,128)S(1)}, u32[]{:S(2)}, u32[]{:S(2)}) collective-permute-start(f32[512,256]{0,1:T(8,128)} %reduce-scatter.5.cloned.1.call-done), channel_id=1, source_target_pairs={{0,16},{1,17},{2,18},{3,19},{4,20},{5,21},{6,22},{7,23},{8,24},{9,... | collective-permute-start | bytes 1572872 | tf_op jit(solution)/shard_map/ppermute | solution.py:12
  139.0 5.8 %collective-permute-start.7 = (bf16[512,256]{0,1:T(8,128)(2,1)S(1)}, bf16[512,256]{0,1:T(8,128)(2,1)S(1)}, u32[]{:S(2)}, u32[]{:S(2)}) collective-permute-start(bf16[512,256]{0,1:T(8,128)(2,1)S(1)} %collective-permute-done.6), channel_id=1, source_target_pairs={{0,1},{1,2},{2,3},{3,0},{4,5},{5,6},{6,7},{7,4},{8,9},{9,10},{10,1... | collective-permute-start | bytes 786440 | tf_op jit(solution)/shard_map/ppermute | solution.py:38
  144.8 5.8 %collective-permute-start.8 = (bf16[512,256]{0,1:T(8,128)(2,1)S(1)}, bf16[512,256]{0,1:T(8,128)(2,1)S(1)}, u32[]{:S(2)}, u32[]{:S(2)}) collective-permute-start(bf16[512,256]{0,1:T(8,128)(2,1)S(1)} %collective-permute-done.7), channel_id=1, source_target_pairs={{0,1},{1,2},{2,3},{3,0},{4,5},{5,6},{6,7},{7,4},{8,9},{9,10},{10,1... | collective-permute-start | bytes 786440 | tf_op jit(solution)/shard_map/ppermute | solution.py:38
  149.8 74.6 %reduce-scatter.11.cloned.1.call-start = ((), (), s32[]{:S(2)}) async-start(), calls=%async_computation.8 | async-start | bytes 2621440 | tf_op jit(solution)/shard_map/reduce_scatter | solution.py:45
  165.4 92.4 %reduce-scatter.9.cloned.1.call-start = ((), (), s32[]{:S(2)}) async-start(), calls=%async_computation.7 | async-start | bytes 2621440 | tf_op jit(solution)/shard_map/reduce_scatter | solution.py:23
  178.9 6.2 %copy-start.7 = (bf16[2048,256]{0,1:T(8,128)(2,1)S(1)}, bf16[2048,256]{0,1:T(8,128)(2,1)}, u32[]{:S(2)}) copy-start(bf16[2048,256]{0,1:T(8,128)(2,1)} %all-gather.4.cloned.1.call-done) | copy-start | bytes 3145732
  224.4 48.2 %copy-start.2 = (f32[512,256]{0,1:T(8,128)S(1)}, f32[512,256]{0,1:T(8,128)}, u32[]{:S(2)}) copy-start(f32[512,256]{0,1:T(8,128)} %reduce-scatter.11.cloned.1.call-done) | copy-start | bytes 1572868
  224.4 36.7 %collective-permute-start.9 = (f32[512,256]{0,1:T(8,128)}, f32[512,256]{0,1:T(8,128)S(1)}, u32[]{:S(2)}, u32[]{:S(2)}) collective-permute-start(f32[512,256]{0,1:T(8,128)} %reduce-scatter.11.cloned.1.call-done), channel_id=1, source_target_pairs={{16,0},{17,1},{18,2},{19,3},{20,4},{21,5},{22,6},{23,7},{24,8},{25... | collective-permute-start | bytes 1572872 | tf_op jit(solution)/shard_map/ppermute | solution.py:12
  257.7 14.9 %collective-permute-start.4 = (f32[512,256]{0,1:T(8,128)}, f32[512,256]{0,1:T(8,128)S(1)}, u32[]{:S(2)}, u32[]{:S(2)}) collective-permute-start(f32[512,256]{0,1:T(8,128)} %reduce-scatter.9.cloned.1.call-done), channel_id=1, source_target_pairs={{0,16},{1,17},{2,18},{3,19},{4,20},{5,21},{6,22},{7,23},{8,24},{9,... | collective-permute-start | bytes 1572872 | tf_op jit(solution)/shard_map/ppermute | solution.py:12
Sparse Core Ops, SparseCore 0:
  22.5 30.3 all-gather.5
  55.1 43.3 reduce-scatter.6
  101.2 30.7 reduce-scatter.4
  149.9 28.9 all-gather.3
  181.0 43.3 reduce-scatter.10
  227.0 30.7 reduce-scatter.8
